TPU v7x, 32 devices: a whole 2x2x4 slice. The times are simulated.
32 devices in a mesh: groups: 2 (over y), seq: 8 (over z, x), section: 2 (over core).
Axes of the slice: x: 2, y: 2, z: 4, core: 2. Of those that a mesh axis runs over, the one named last changes fastest.
Arguments:
- skip_in: bfloat16 [2, 1024, 1536], P('groups', 'seq'), parts along dimension 0, may hold values from -6 to 6
- attn_gain: float32 [1536], replicated, may hold values from 0.25 to 1.75
- query_weight: bfloat16 [1536, 1024], P(None, 'section'), may hold values from -0.625 to 0.625
- kv_weight: bfloat16 [1536, 256], replicated, may hold values from -0.15625 to 0.15625
- pair_bias: float32 [2, 8, 32, 32], P('groups', 'section', 'seq'), parts along dimension 0, may hold values from -12 to 400
- out_weight: bfloat16 [1024, 1536], P('section'), may hold values from -0.1875 to 0.1875
- dec_gain: float32 [1536], replicated, may hold values from 0.25 to 1.75
- dec_weight: bfloat16 [5, 1536, 768], P(None, 'seq', 'section'), may hold values from -0.0625 to 0.0625
- dec_bias: float32 [768], P('section'), may hold values from -3 to 3
Outputs:
- decoded: bfloat16 [2, 1024, 768], P('groups', 'seq', 'section'), parts along dimension 0
There are 2 independent parts, one for each index of `groups`. A program takes and returns all parts, laid end to end along the dimension named above; an argument that names none is the same for every part. Nothing has to cross between parts.
All inputs are finite; a program needn't handle non-finite values.
Results may differ from a plain program's by a relative error of at most 0.0095.
Values may be sent and summed in bfloat16 or wider, within the bound.
No kernel may reach another device: no remote copies, remote signals or barrier semaphores. Data moves between devices by JAX's collectives and lax.ppermute only.
A program may use at most 64 MiB of HBM per device.

v0:
```python
import math
import jax
import jax.numpy as jnp
from jax import lax
from jax.sharding import PartitionSpec as P

HEAD = 128
KW = 5
PAIR = 16


def extended(block, sides, width):
    for axis, dim in sides:
        count = lax.axis_size(axis)
        forward = [(i, i + 1) for i in range(count - 1)]
        backward = [(target, source) for source, target in forward]
        low = lax.ppermute(
            lax.slice_in_dim(block, block.shape[dim] - width, None, axis=dim), axis, forward
        )
        high = lax.ppermute(lax.slice_in_dim(block, 0, width, axis=dim), axis, backward)
        block = jnp.concatenate([low, block, high], axis=dim)
    return block


def norm_scale(values_in, gain):
    wide = values_in.astype(jnp.float32)
    return wide * lax.rsqrt(jnp.mean(wide * wide, axis=-1, keepdims=True) + 1e-06) * gain


def body(
    skip_in,
    attn_gain,
    query_weight,
    kv_weight,
    pair_bias,
    out_weight,
    dec_gain,
    dec_weight,
    dec_bias,
):
    seq_count, local_rows, channels = skip_in.shape
    half_rows = local_rows // 2
    local_heads = query_weight.shape[1] // HEAD
    logit_scale = 1.0 / math.sqrt(HEAD)
    pooled = jnp.max(skip_in.reshape(seq_count, half_rows, 2, channels), axis=2)
    normed = norm_scale(pooled, attn_gain).astype(jnp.bfloat16)
    flattened = normed.reshape(seq_count * half_rows, channels)
    query_rows = jnp.dot(flattened, query_weight, preferred_element_type=jnp.float32).astype(
        jnp.bfloat16
    )
    query_rows = query_rows.reshape(seq_count, half_rows, local_heads, HEAD)
    row_bias = jnp.repeat(pair_bias, PAIR, axis=2)
    row_bias = jnp.pad(row_bias, ((0, 0), (0, 0), (0, 0), (0, 2)))
    quarter = half_rows // 2
    own_rows = lax.dynamic_slice_in_dim(normed, lax.axis_index("section") * quarter, quarter, 1)
    key_values = jnp.dot(
        own_rows.reshape(seq_count * quarter, channels),
        kv_weight,
        preferred_element_type=jnp.float32,
    )
    key_values = key_values.astype(jnp.bfloat16).reshape(seq_count, quarter, 2 * HEAD)
    piece = lax.all_gather(key_values, ("seq", "section"), axis=1, tiled=True)
    start = jnp.int32(0)
    running_max = jnp.full((seq_count, local_heads, half_rows), -1e30, jnp.float32)
    running_sum = jnp.zeros((seq_count, local_heads, half_rows), jnp.float32)
    weighted = jnp.zeros((seq_count, local_heads, half_rows, HEAD), jnp.float32)
    piece_rows = piece.shape[1]
    block_size = min(piece_rows, 2048)
    for offset in range(0, piece_rows, block_size):
        piece_len = min(block_size, piece_rows - offset)
        sub_piece = piece[:, offset : offset + piece_len]
        key_portion = sub_piece[:, :, :HEAD]
        value_part = sub_piece[:, :, HEAD:]
        first_row = start + offset
        blocks = lax.dynamic_slice_in_dim(row_bias, first_row // PAIR, piece_len // PAIR + 2, 3)
        spread = jnp.repeat(blocks, PAIR, axis=3)
        key_bias = lax.dynamic_slice_in_dim(spread, first_row % PAIR, piece_len, 3)
        scores = (
            jnp.einsum(
                "wtzj,wgj->wztg", query_rows, key_portion, preferred_element_type=jnp.float32
            )
            * logit_scale
            + key_bias
        )
        new_max = jnp.maximum(running_max, jnp.max(scores, axis=-1))
        rescale = jnp.exp(running_max - new_max)
        exponent_scores = jnp.exp(scores - new_max[..., None])
        running_sum = running_sum * rescale + jnp.sum(exponent_scores, axis=-1)
        weighted = weighted * rescale[..., None] + jnp.einsum(
            "umrl,ult->umrt",
            exponent_scores.astype(jnp.bfloat16),
            value_part,
            preferred_element_type=jnp.float32,
        )
        running_max = new_max
    folded = (running_max, running_sum, weighted)
    running_max, running_sum, weighted = folded
    context = (weighted / running_sum[..., None]).astype(jnp.bfloat16)
    context = jnp.transpose(context, (0, 2, 1, 3)).reshape(
        seq_count * half_rows, local_heads * HEAD
    )
    partial_value = jnp.dot(context, out_weight, preferred_element_type=jnp.float32).reshape(
        seq_count, half_rows, channels
    )
    summed = lax.psum(partial_value.astype(jnp.bfloat16), "section").astype(jnp.float32)
    attended = (pooled.astype(jnp.float32) + summed).astype(jnp.bfloat16)
    joined = (
        jnp.repeat(attended, 2, axis=1).astype(jnp.float32) + skip_in.astype(jnp.float32)
    ).astype(jnp.bfloat16)
    activated = jax.nn.gelu(norm_scale(joined, dec_gain)).astype(jnp.bfloat16)
    padded = extended(activated, (("seq", 1),), KW // 2)
    out_half = dec_weight.shape[2]
    piece = lax.all_gather(dec_weight, "seq", axis=1, tiled=True)
    piece_rows = piece.shape[1]
    stacked = jnp.concatenate(
        [padded[:, tap_index : tap_index + local_rows] for tap_index in range(KW)], axis=2
    )
    stacked = stacked.reshape(seq_count * local_rows, KW * piece_rows)
    convolved = jnp.dot(
        stacked, piece.reshape(KW * piece_rows, out_half), preferred_element_type=jnp.float32
    )
    residual = lax.dynamic_slice_in_dim(joined, lax.axis_index("section") * out_half, out_half, 2)
    decoded = (
        convolved.reshape(seq_count, local_rows, out_half) + dec_bias + residual.astype(jnp.float32)
    )
    return decoded.astype(jnp.bfloat16)


def solution(mesh):
    return jax.shard_map(
        body,
        mesh=mesh,
        in_specs=(
            P("groups", "seq", None),
            P(),
            P(None, "section"),
            P(),
            P("groups", "section", "seq", None),
            P("section", None),
            P(),
            P(None, "seq", "section"),
            P("section"),
        ),
        out_specs=P("groups", "seq", "section"),
        check_vma=False,
    )
```

profile of v0, /device:TPU:0, one launch (start us, length us, event | category | flops | bytes accessed | tf_op | source)
XLA Modules:
  0.0 150.7 jit_solution(8483585687084230014)
XLA Ops:
  7.4 0.0 copy-start
  7.4 0.0 all-reduce.3.cloned.1.call-start
  7.4 2.0 %reshape.220 = bf16[64,2,1536]{2,1,0:T(2,128)(2,1)} reshape(bf16[1,128,1536]{2,1,0:T(8,128)(2,1)} %param.9) | data formatting | bytes 786432 | tf_op jit(solution)/shard_map/reshape | solution.py:45
  9.4 2.0 %reduce_max.18 = bf16[64,1536]{1,0:T(8,128)(2,1)S(1)} reduce(bf16[64,2,1536]{2,1,0:T(2,128)(2,1)} %reshape.220, bf16[]{:T(256)} %constant.24.clone.1), dimensions={1}, to_apply=%region_0.0 | reduce | flops 98304 | bytes 589826 | tf_op jit(solution)/shard_map/reduce_max | solution.py:45
  11.4 0.0 copy-start.4
  11.4 0.1 fusion.37
  11.5 0.8 convert_bitcast_fusion
  12.3 0.1 dynamic-slice.1
  12.4 0.0 copy-done.2
  12.4 1.5 %convolution_convert_fusion.2 = bf16[32,256]{1,0:T(8,128)(2,1)S(1)} fusion(bf16[1536,256]{1,0:T(8,128)(2,1)} %param.12, f32[1,64,1536]{2,1,0:T(8,128)} %convert_bitcast_fusion, s32[]{:T(128)S(6)} %select_n.15, f32[1536]{0:T(1024)S(1)} %copy-done.2, f32[32]{0:T(128)S(1)} %dynamic-slice.1), kind=kOutput, calls=%fused_computation.18 | convolution fusion | flops 25321472 | bytes 1005700 | tf_op jit(solution)/shard_map/dot_general | solution.py:56
  13.9 25.2 %all-gather = bf16[512,256]{1,0:T(8,128)(2,1)} all-gather(bf16[32,256]{1,0:T(8,128)(2,1)S(1)} %convolution_convert_fusion.2), channel_id=2, replica_groups=mesh['groups'=2,'seq'=8,'section'=2] {'seq','section'}, dimensions={0}, use_global_device_ids=true | all-gather | bytes 278528 | tf_op jit(solution)/shard_map/all_gather | solution.py:62
  39.1 0.0 copy-done.1
  39.1 0.4 fusion.19
  39.6 0.0 copy-done.4
  39.6 0.1 copy.16
  39.7 0.1 broadcast_in_dim.31
  39.8 0.1 slice.41
  39.9 0.3 copy.19
  40.2 1.2 fusion.63
  41.4 0.2 fusion.31
  41.7 1.2 fusion.20
  42.9 0.1 copy.18
  42.9 0.0 copy-done
  42.9 1.1 fusion
  44.0 0.0 all-reduce.3.cloned.1.call-update
  44.0 0.0 all-gather.3.cloned.1.call-start
  44.1 0.5 all-gather.3.cloned.1.call-update
  44.6 15.0 %all-reduce.3.cloned.1.call-done = bf16[1,64,1536]{2,1,0:T(8,128)(2,1)} async-done(((bf16[1,64,1536]{2,1,0:T(8,128)(2,1)}), bf16[1,64,1536]{2,1,0:T(8,128)(2,1)}) %all-reduce.3.cloned.1.call-update) | async-done | bytes 196624 | tf_op jit(solution)/shard_map/psum | solution.py:105
  59.6 1.0 fusion.46
  60.6 0.0 copy-start.3
  60.6 0.3 broadcast_in_dim.34
  60.9 0.5 convert_element_type.120
  61.4 1.2 fusion.21
  62.6 0.0 copy-done.3
  62.6 0.4 fusion.25
  63.0 3.6 %collective-permute-start = (bf16[1,2,1536]{2,1,0:T(2,128)(2,1)S(1)}, bf16[1,2,1536]{2,1,0:T(2,128)(2,1)S(1)}, u32[]{:S(2)}, u32[]{:S(2)}) collective-permute-start(bf16[1,2,1536]{2,1,0:T(2,128)(2,1)S(1)} %get-tuple-element.8), channel_id=1, source_target_pairs={{0,2},{2,4},{4,6},{6,8},{8,10},{10,12},{12,14},{1,3},{3,5},{5,7},{... | collective-permute-start | bytes 18440 | tf_op jit(solution)/shard_map/ppermute | solution.py:17
  66.7 0.0 copy-start.5
  66.7 1.3 collective-permute-start.1
  68.0 0.0 collective-permute-done
  68.0 0.8 fusion.36
  68.8 0.9 fusion.41
  69.7 1.2 constant_dynamic-update-slice_fusion
  70.9 1.3 collective-permute-done.1
  72.2 0.9 fusion.34
  73.1 0.9 fusion.40
  74.0 64.1 %all-gather.3.cloned.1.call-done = bf16[5,1536,384]{2,1,0:T(8,128)(2,1)} async-done(((bf16[5,192,384]{2,1,0:T(8,128)(2,1)}), bf16[5,1536,384]{2,1,0:T(8,128)(2,1)}) %all-gather.3.cloned.1.call-update) | async-done | bytes 5898256 | tf_op jit(solution)/shard_map/all_gather | solution.py:113
  138.1 0.0 copy-done.5
  138.1 5.1 %fusion.14 = bf16[1,128,384]{2,1,0:T(8,128)(2,1)} fusion(bf16[7680,384]{1,0:T(8,128)(2,1)} %bitcast.79, bf16[1,128,7680]{2,1,0:T(8,128)(2,1)} %fusion.40, bf16[1,128,1536]{2,1,0:T(8,128)(2,1)S(1)} %get-tuple-element.6, s32[]{:T(128)S(6)} %select_n.16, f32[384]{0:T(512)S(1)} %copy-done.5), kind=kOutput, calls=%fused_computation.11 | convolution fusion | flops 755171328 | bytes 8062468 | tf_op jit(solution)/shard_map/dot_general | solution.py:119
  (9 shorter events, 0.1 us)
Async XLA Ops:
  7.4 35.6 %copy-start = (bf16[512,1536]{1,0:T(8,128)(2,1)S(1)}, bf16[512,1536]{1,0:T(8,128)(2,1)}, u32[]{:S(2)}) copy-start(bf16[512,1536]{1,0:T(8,128)(2,1)} %param.14) | copy-start | bytes 4718596
  7.4 5.0 %copy-start.2 = (f32[1536]{0:T(1024)S(1)}, f32[1536]{0:T(1024)}, u32[]{:S(2)}) copy-start(f32[1536]{0:T(1024)} %param.10) | copy-start | bytes 18436
  7.4 31.7 %copy-start.1 = (bf16[1536,512]{1,0:T(8,128)(2,1)S(1)}, bf16[1536,512]{1,0:T(8,128)(2,1)}, u32[]{:S(2)}) copy-start(bf16[1536,512]{1,0:T(8,128)(2,1)} %param.11) | copy-start | bytes 4718596
  7.4 52.2 %all-reduce.3.cloned.1.call-start = ((), (), s32[]{:S(2)}) async-start(), calls=%async_computation | async-start | bytes 393216 | tf_op jit(solution)/shard_map/psum | solution.py:105
  11.4 28.2 %copy-start.4 = (f32[1,4,4,32]{3,2,1,0:T(4,128)S(1)}, f32[1,4,4,32]{3,2,1,0:T(4,128)}, u32[]{:S(2)}) copy-start(f32[1,4,4,32]{3,2,1,0:T(4,128)} %param.13) | copy-start | bytes 6148
  44.0 94.0 %all-gather.3.cloned.1.call-start = ((), (), s32[]{:S(2)}) async-start(), calls=%async_computation.1 | async-start | bytes 6635520 | tf_op jit(solution)/shard_map/all_gather | solution.py:113
  60.6 2.1 %copy-start.3 = (f32[1536]{0:T(1024)S(1)}, f32[1536]{0:T(1024)}, u32[]{:S(2)}) copy-start(f32[1536]{0:T(1024)} %param.15) | copy-start | bytes 18436
  63.0 5.0 %collective-permute-start = (bf16[1,2,1536]{2,1,0:T(2,128)(2,1)S(1)}, bf16[1,2,1536]{2,1,0:T(2,128)(2,1)S(1)}, u32[]{:S(2)}, u32[]{:S(2)}) collective-permute-start(bf16[1,2,1536]{2,1,0:T(2,128)(2,1)S(1)} %get-tuple-element.8), channel_id=1, source_target_pairs={{0,2},{2,4},{4,6},{6,8},{8,10},{10,12},{12,14},{1,3},{3,5},{5,7},{... | collective-permute-start | bytes 18440 | tf_op jit(solution)/shard_map/ppermute | solution.py:17
  66.7 71.4 %copy-start.5 = (f32[384]{0:T(512)S(1)}, f32[384]{0:T(512)}, u32[]{:S(2)}) copy-start(f32[384]{0:T(512)} %param.17) | copy-start | bytes 4612
  66.7 5.5 %collective-permute-start.1 = (bf16[1,2,1536]{2,1,0:T(2,128)(2,1)S(1)}, bf16[1,2,1536]{2,1,0:T(2,128)(2,1)S(1)}, u32[]{:S(2)}, u32[]{:S(2)}) collective-permute-start(bf16[1,2,1536]{2,1,0:T(2,128)(2,1)S(1)} %get-tuple-element.7), channel_id=1, source_target_pairs={{2,0},{4,2},{6,4},{8,6},{10,8},{12,10},{14,12},{3,1},{5,3},{7,5},{... | collective-permute-start | bytes 18440 | tf_op jit(solution)/shard_map/ppermute | solution.py:20
Sparse Core Ops, SparseCore 0:
  44.2 15.3 all-reduce.2
Sparse Core Ops, SparseCore 1:
  46.7 91.3 all-gather.2
where the time goes:
time: 151 us
  waiting for transfers between devices  81 us (54%)
  blocking collectives  25.2 us (17%)
  between operations  15 us (10%)
  matrix products  10.6 us (7%)
  other arithmetic  10.3 us (7%)
  starting transfers between devices  4.96 us (3%)
  local copies, waits for them, and re-layouts  3.61 us (2%)
    all_gather x1, waiting for transfers between devices, body(): piece = lax.all_gather(dec_weight, 'seq', axis=1, tiled=True)  64.1 us
    all_gather x1, blocking collectives, body(): piece = lax.all_gather(key_values, ('seq', 'section'), axis=1, tiled=True)  25.2 us
    psum x1, waiting for transfers between devices, body(): lax.psum(partial_value.astype(jnp.bfloat16), 'section').astype(jnp.float32)  15 us
    dot_general x1, matrix products, body(): jnp.dot(stacked, piece.reshape(KW * piece_rows, out_half), preferred_elem...  5.14 us
    unnamed x4, other arithmetic  3.74 us
    ppermute x1, starting transfers between devices, extended(): lax.ppermute(lax.slice_in_dim(block, block.shape[dim] - width, None, axis...  3.62 us
  transfers between devices with their start and end apart: 4, of which 3 were waited for; matrix products, arithmetic and copies ran while one was open for 5% of the time, Pallas kernels for 0%

commit v1 on v0

--- a/solution.py
+++ b/solution.py
@@ -7,6 +7,19 @@
 HEAD = 128
 KW = 5
 PAIR = 16
+
+
+def ring_gather(value, axis, dim):
+    ways = lax.axis_size(axis)
+    up = [(d, (d + 1) % ways) for d in range(ways)]
+    down = [(d, (d - 1) % ways) for d in range(ways)]
+    earlier, later = ([value], [value])
+    for _ in range(ways // 2):
+        earlier.append(lax.ppermute(earlier[-1], axis, up))
+    for _ in range((ways - 1) // 2):
+        later.append(lax.ppermute(later[-1], axis, down))
+    line = jnp.concatenate([*earlier[::-1], *later[1:]], axis=dim)
+    return jnp.roll(line, (lax.axis_index(axis) - ways // 2) * value.shape[dim], axis=dim)
 
 
 def extended(block, sides, width):
@@ -110,7 +123,7 @@
     activated = jax.nn.gelu(norm_scale(joined, dec_gain)).astype(jnp.bfloat16)
     padded = extended(activated, (("seq", 1),), KW // 2)
     out_half = dec_weight.shape[2]
-    piece = lax.all_gather(dec_weight, "seq", axis=1, tiled=True)
+    piece = ring_gather(dec_weight, "seq", 1)
     piece_rows = piece.shape[1]
     stacked = jnp.concatenate(
         [padded[:, tap_index : tap_index + local_rows] for tap_index in range(KW)], axis=2

time: 151 us -> 181 us (1.20)
  local copies, waits for them, and re-layouts: 3.61 us -> 31.9 us
  starting transfers between devices: 4.96 us -> 14.1 us
  other arithmetic: 10.3 us -> 5.56 us
  matrix products: 10.6 us -> 6.96 us
  waiting for transfers between devices: 81 us -> 83.6 us
    all_gather x1 -> x0, waiting for transfers between devices: 64.1 us -> none  [body(): piece = lax.all_gather(dec_weight, 'seq', axis=1, tiled=True)]
    ppermute x0 -> x7, waiting for transfers between devices: none -> 56.8 us  [the longest x3 37.7 us: ring_gather(): later.append(lax.ppermute(later[-1], axis, down))]
    unnamed x13 -> x22, local copies, waits for them, and re-layouts: 0.34 us -> 23.7 us
    ppermute x1, waiting for transfers between devices: 0.01 us -> 11.7 us  [extended(): lax.ppermute(lax.slice_in_dim(block, block.shape[dim] - width, None, axis...]
    ppermute x0 -> x7, starting transfers between devices: none -> 9.56 us  [the longest x3 4.84 us: ring_gather(): later.append(lax.ppermute(later[-1], axis, down))]
    dynamic_slice x0 -> x1, local copies, waits for them, and re-layouts: none -> 4.16 us  [ring_gather(): jnp.roll(line, (lax.axis_index(axis) - ways // 2) * value.shape[dim], axi...]
    dot_general x1, matrix products: 5.14 us -> 1.9 us  [body(): jnp.dot(stacked, piece.reshape(KW * piece_rows, out_half), preferred_elem...]
    unnamed x4, other arithmetic: 3.74 us -> 0.69 us
  transfers between devices with their start and end apart: 4 -> 10, of which waited for: 3 -> 6; matrix products, arithmetic and copies ran while one was open for 5% -> 14% of each run, Pallas kernels for 0% -> 0%
where the time goes in v1:
time: 181 us
  waiting for transfers between devices  83.6 us (46%)
  local copies, waits for them, and re-layouts  31.9 us (18%)
  blocking collectives  25 us (14%)
  starting transfers between devices  14.1 us (8%)
  between operations  13.7 us (8%)
  matrix products  6.96 us (4%)
  other arithmetic  5.56 us (3%)
    ppermute x3, waiting for transfers between devices, ring_gather(): later.append(lax.ppermute(later[-1], axis, down))  37.7 us
    all_gather x1, blocking collectives, body(): piece = lax.all_gather(key_values, ('seq', 'section'), axis=1, tiled=True)  25 us
    unnamed x22, local copies, waits for them, and re-layouts  23.7 us
    ppermute x4, waiting for transfers between devices, ring_gather(): earlier.append(lax.ppermute(earlier[-1], axis, up))  19.2 us
    psum x1, waiting for transfers between devices, body(): lax.psum(partial_value.astype(jnp.bfloat16), 'section').astype(jnp.float32)  15.1 us
    ppermute x1, waiting for transfers between devices, extended(): lax.ppermute(lax.slice_in_dim(block, block.shape[dim] - width, None, axis...  11.7 us
    ppermute x3, starting transfers between devices, ring_gather(): later.append(lax.ppermute(later[-1], axis, down))  4.84 us
    ppermute x4, starting transfers between devices, ring_gather(): earlier.append(lax.ppermute(earlier[-1], axis, up))  4.72 us
  transfers between devices with their start and end apart: 10, of which 6 were waited for; matrix products, arithmetic and copies ran while one was open for 14% of the time, Pallas kernels for 0%

profile of v1, /device:TPU:0, one launch (start us, length us, event | category | flops | bytes accessed | tf_op | source)
XLA Modules:
  0.0 180.8 jit_solution(9574251749423127641)
XLA Ops:
  6.5 2.9 %collective-permute-start.2 = (bf16[5,192,384]{2,1,0:T(8,128)(2,1)}, bf16[5,192,384]{2,1,0:T(8,128)(2,1)}, u32[]{:S(2)}, u32[]{:S(2)}) collective-permute-start(bf16[5,192,384]{2,1,0:T(8,128)(2,1)} %param.16), channel_id=1, source_target_pairs={{0,2},{2,4},{4,6},{6,8},{8,10},{10,12},{12,14},{14,0},{1,3},{3,5},... | collective-permute-start | bytes 2211848 | tf_op jit(solution)/shard_map/ppermute | solution.py:18
  9.5 1.1 reshape.220
  10.6 1.0 reduce_max.18
  11.8 0.8 convert_bitcast_fusion
  12.6 0.7 broadcast_in_dim.29
  13.6 0.3 copy.19
  14.0 1.9 %fusion.19 = bf16[8,4,8,128]{3,2,1,0:T(8,128)(2,1)S(1)} fusion(bf16[1536,512]{1,0:T(8,128)(2,1)} %param.11, bf16[64,1536]{1,0:T(8,128)(2,1)S(1)} %reduce_max.18, f32[1536]{0:T(1024)} %param.10, f32[64]{0:T(128)S(1)} %add_rsqrt_fusion.1), kind=kOutput, calls=%fused_computation.16 | convolution fusion | flops 101089280 | bytes 1841408 | tf_op jit(solution)/shard_map/dot_general | solution.py:61
  15.9 1.5 convolution_convert_fusion.2
  17.4 25.0 %all-gather = bf16[512,256]{1,0:T(8,128)(2,1)S(1)} all-gather(bf16[32,256]{1,0:T(8,128)(2,1)S(1)} %convolution_convert_fusion.2), channel_id=2, replica_groups=mesh['groups'=2,'seq'=8,'section'=2] {'seq','section'}, dimensions={0}, use_global_device_ids=true | all-gather | bytes 278528 | tf_op jit(solution)/shard_map/all_gather | solution.py:75
  42.4 0.3 fusion.63
  42.9 0.3 fusion.20
  43.3 1.1 fusion
  44.4 0.4 collective-permute-start.6
  44.8 15.1 %all-reduce.3.cloned.1.call-done = bf16[1,64,1536]{2,1,0:T(8,128)(2,1)} async-done(((bf16[1,64,1536]{2,1,0:T(8,128)(2,1)}), bf16[1,64,1536]{2,1,0:T(8,128)(2,1)}) %all-reduce.3.cloned.1.call-update) | async-done | bytes 196624 | tf_op jit(solution)/shard_map/psum | solution.py:118
  59.9 1.0 fusion.46
  60.9 0.3 broadcast_in_dim.34
  61.2 0.5 convert_element_type.120
  61.8 1.8 collective-permute-start.3
  63.5 1.2 fusion.21
  64.7 0.4 fusion.25
  65.1 18.4 %collective-permute-done.3 = bf16[5,192,384]{2,1,0:T(8,128)(2,1)} collective-permute-done((bf16[5,192,384]{2,1,0:T(8,128)(2,1)}, bf16[5,192,384]{2,1,0:T(8,128)(2,1)}, u32[]{:S(2)}, u32[]{:S(2)}) %collective-permute-start.3) | collective-permute-done | bytes 737312 | tf_op jit(solution)/shard_map/ppermute | solution.py:18
  83.6 3.3 %collective-permute-start = (bf16[1,2,1536]{2,1,0:T(2,128)(2,1)S(1)}, bf16[1,2,1536]{2,1,0:T(2,128)(2,1)S(1)}, u32[]{:S(2)}, u32[]{:S(2)}) collective-permute-start(bf16[1,2,1536]{2,1,0:T(2,128)(2,1)S(1)} %get-tuple-element.8), channel_id=1, source_target_pairs={{0,2},{2,4},{4,6},{6,8},{8,10},{10,12},{12,14},{1,3},{3,5},{5,7},{... | collective-permute-start | bytes 18440 | tf_op jit(solution)/shard_map/ppermute | solution.py:30
  86.9 1.3 collective-permute-start.1
  88.2 11.7 %collective-permute-done = bf16[1,2,1536]{2,1,0:T(2,128)(2,1)S(1)} collective-permute-done((bf16[1,2,1536]{2,1,0:T(2,128)(2,1)S(1)}, bf16[1,2,1536]{2,1,0:T(2,128)(2,1)S(1)}, u32[]{:S(2)}, u32[]{:S(2)}) %collective-permute-start) | collective-permute-done | bytes 6176 | tf_op jit(solution)/shard_map/ppermute | solution.py:30
  100.1 3.8 %collective-permute-start.7 = (bf16[5,192,384]{2,1,0:T(8,128)(2,1)}, bf16[5,192,384]{2,1,0:T(8,128)(2,1)S(1)}, u32[]{:S(2)}, u32[]{:S(2)}) collective-permute-start(bf16[5,192,384]{2,1,0:T(8,128)(2,1)} %collective-permute-done.6), channel_id=1, source_target_pairs={{0,14},{2,0},{4,2},{6,4},{8,6},{10,8},{12,10},{14,12},{1,15},{3,1}... | collective-permute-start | bytes 2211848 | tf_op jit(solution)/shard_map/ppermute | solution.py:20
  103.8 0.7 collective-permute-done.4
  104.5 0.4 constant_dynamic-update-slice_fusion
  105.2 31.0 %collective-permute-done.7 = bf16[5,192,384]{2,1,0:T(8,128)(2,1)S(1)} collective-permute-done((bf16[5,192,384]{2,1,0:T(8,128)(2,1)}, bf16[5,192,384]{2,1,0:T(8,128)(2,1)S(1)}, u32[]{:S(2)}, u32[]{:S(2)}) %collective-permute-start.7) | collective-permute-done | bytes 737312 | tf_op jit(solution)/shard_map/ppermute | solution.py:20
  136.2 0.7 collective-permute-start.8
  136.8 1.0 constant_dynamic-update-slice_fusion.16
  137.8 1.0 constant_dynamic-update-slice_fusion.15
  138.7 2.1 %constant_dynamic-update-slice_fusion.14 = bf16[5,3072,384]{2,1,0:T(8,128)(2,1)} fusion(bf16[5,3072,384]{2,1,0:T(8,128)(2,1)} %constant_dynamic-update-slice_fusion.15, bf16[5,192,384]{2,1,0:T(8,128)(2,1)} %collective-permute-done.3), kind=kLoop, calls=%fused_computation.87 | loop fusion | bytes 1474560
  140.8 2.1 %constant_dynamic-update-slice_fusion.13 = bf16[5,3072,384]{2,1,0:T(8,128)(2,1)} fusion(bf16[5,3072,384]{2,1,0:T(8,128)(2,1)} %constant_dynamic-update-slice_fusion.14, bf16[5,192,384]{2,1,0:T(8,128)(2,1)} %collective-permute-done.2), kind=kLoop, calls=%fused_computation.86 | loop fusion | bytes 1474560
  142.9 2.1 %constant_dynamic-update-slice_fusion.12 = bf16[5,3072,384]{2,1,0:T(8,128)(2,1)} fusion(bf16[5,3072,384]{2,1,0:T(8,128)(2,1)} %constant_dynamic-update-slice_fusion.13, bf16[5,192,384]{2,1,0:T(8,128)(2,1)} %param.16), kind=kLoop, calls=%fused_computation.85 | loop fusion | bytes 1474560
  145.0 2.1 %constant_dynamic-update-slice_fusion.11 = bf16[5,3072,384]{2,1,0:T(8,128)(2,1)} fusion(bf16[5,3072,384]{2,1,0:T(8,128)(2,1)} %constant_dynamic-update-slice_fusion.12, bf16[5,192,384]{2,1,0:T(8,128)(2,1)} %collective-permute-done.6), kind=kLoop, calls=%fused_computation.84 | loop fusion | bytes 1474560
  147.0 0.9 constant_dynamic-update-slice_fusion.10
  148.0 6.7 %collective-permute-done.8 = bf16[5,192,384]{2,1,0:T(8,128)(2,1)S(1)} collective-permute-done((bf16[5,192,384]{2,1,0:T(8,128)(2,1)S(1)}, bf16[5,192,384]{2,1,0:T(8,128)(2,1)S(1)}, u32[]{:S(2)}, u32[]{:S(2)}) %collective-permute-start.8) | collective-permute-done | bytes 737312 | tf_op jit(solution)/shard_map/ppermute | solution.py:20
  154.6 1.0 constant_dynamic-update-slice_fusion.9
  155.6 1.0 constant_dynamic-update-slice_fusion.8
  156.6 1.0 constant_dynamic-update-slice_fusion.7
  157.6 2.1 %constant_dynamic-update-slice_fusion.6 = bf16[5,3072,384]{2,1,0:T(8,128)(2,1)} fusion(bf16[5,3072,384]{2,1,0:T(8,128)(2,1)} %constant_dynamic-update-slice_fusion.7, bf16[5,192,384]{2,1,0:T(8,128)(2,1)} %collective-permute-done.3), kind=kLoop, calls=%fused_computation.79 | loop fusion | bytes 1474560
  159.7 2.1 %constant_dynamic-update-slice_fusion.5 = bf16[5,3072,384]{2,1,0:T(8,128)(2,1)} fusion(bf16[5,3072,384]{2,1,0:T(8,128)(2,1)} %constant_dynamic-update-slice_fusion.6, bf16[5,192,384]{2,1,0:T(8,128)(2,1)} %collective-permute-done.2), kind=kLoop, calls=%fused_computation.78 | loop fusion | bytes 1474560
  161.8 2.1 %constant_dynamic-update-slice_fusion.4 = bf16[5,3072,384]{2,1,0:T(8,128)(2,1)} fusion(bf16[5,3072,384]{2,1,0:T(8,128)(2,1)} %constant_dynamic-update-slice_fusion.5, bf16[5,192,384]{2,1,0:T(8,128)(2,1)} %param.16), kind=kLoop, calls=%fused_computation.77 | loop fusion | bytes 1474560
  163.8 2.1 %constant_dynamic-update-slice_fusion.3 = bf16[5,3072,384]{2,1,0:T(8,128)(2,1)} fusion(bf16[5,3072,384]{2,1,0:T(8,128)(2,1)} %constant_dynamic-update-slice_fusion.4, bf16[5,192,384]{2,1,0:T(8,128)(2,1)} %collective-permute-done.6), kind=kLoop, calls=%fused_computation.76 | loop fusion | bytes 1474560
  165.9 1.0 constant_dynamic-update-slice_fusion.2
  166.9 1.0 constant_dynamic-update-slice_fusion.1
  167.8 4.2 %constant_dynamic-slice_fusion = bf16[5,1536,384]{2,1,0:T(8,128)(2,1)S(1)} fusion(bf16[5,3072,384]{2,1,0:T(8,128)(2,1)} %constant_dynamic-update-slice_fusion.1, s32[]{:T(128)S(6)} %select_n.29), kind=kLoop, calls=%fused_computation.92 | loop fusion | bytes 11796484 | tf_op jit(solution)/shard_map/jit(_roll_dynamic)/dynamic_slice | solution.py:22
  172.0 1.9 %fusion.14 = bf16[1,128,384]{2,1,0:T(8,128)(2,1)} fusion(bf16[7680,384]{1,0:T(8,128)(2,1)S(1)} %bitcast.79, bf16[1,128,7680]{2,1,0:T(8,128)(2,1)S(1)} %fusion.40, bf16[1,128,1536]{2,1,0:T(8,128)(2,1)S(1)} %get-tuple-element.6, s32[]{:T(128)S(6)} %select_n.30, f32[384]{0:T(512)S(1)} %copy-done.2), kind=kOutput, calls=%fused_computation.11 | convolution fusion | flops 755171328 | bytes 8062468 | tf_op jit(solution)/shard_map/dot_general | solution.py:132
  (31 shorter events, 1.3 us)
Async XLA Ops:
  6.5 36.8 %copy-start = (bf16[512,1536]{1,0:T(8,128)(2,1)S(1)}, bf16[512,1536]{1,0:T(8,128)(2,1)}, u32[]{:S(2)}) copy-start(bf16[512,1536]{1,0:T(8,128)(2,1)} %param.14) | copy-start | bytes 4718596
  6.5 58.2 %copy-start.1 = (f32[1536]{0:T(1024)S(1)}, f32[1536]{0:T(1024)}, u32[]{:S(2)}) copy-start(f32[1536]{0:T(1024)} %param.15) | copy-start | bytes 18436
  6.5 53.4 %all-reduce.3.cloned.1.call-start = ((), (), s32[]{:S(2)}) async-start(), calls=%async_computation | async-start | bytes 393216 | tf_op jit(solution)/shard_map/psum | solution.py:118
  6.5 55.2 %collective-permute-start.2 = (bf16[5,192,384]{2,1,0:T(8,128)(2,1)}, bf16[5,192,384]{2,1,0:T(8,128)(2,1)}, u32[]{:S(2)}, u32[]{:S(2)}) collective-permute-start(bf16[5,192,384]{2,1,0:T(8,128)(2,1)} %param.16), channel_id=1, source_target_pairs={{0,2},{2,4},{4,6},{6,8},{8,10},{10,12},{12,14},{14,0},{1,3},{3,5},... | collective-permute-start | bytes 2211848 | tf_op jit(solution)/shard_map/ppermute | solution.py:18
  44.4 55.6 %collective-permute-start.6 = (bf16[5,192,384]{2,1,0:T(8,128)(2,1)}, bf16[5,192,384]{2,1,0:T(8,128)(2,1)}, u32[]{:S(2)}, u32[]{:S(2)}) collective-permute-start(bf16[5,192,384]{2,1,0:T(8,128)(2,1)} %param.16), channel_id=1, source_target_pairs={{0,14},{2,0},{4,2},{6,4},{8,6},{10,8},{12,10},{14,12},{1,15},{3,1}... | collective-permute-start | bytes 2211848 | tf_op jit(solution)/shard_map/ppermute | solution.py:20
  61.8 21.8 %collective-permute-start.3 = (bf16[5,192,384]{2,1,0:T(8,128)(2,1)}, bf16[5,192,384]{2,1,0:T(8,128)(2,1)}, u32[]{:S(2)}, u32[]{:S(2)}) collective-permute-start(bf16[5,192,384]{2,1,0:T(8,128)(2,1)} %collective-permute-done.2), channel_id=1, source_target_pairs={{0,2},{2,4},{4,6},{6,8},{8,10},{10,12},{12,14},{14,0},{1,3},{3,5},... | collective-permute-start | bytes 2211848 | tf_op jit(solution)/shard_map/ppermute | solution.py:18
  83.6 21.0 %collective-permute-start.4 = (bf16[5,192,384]{2,1,0:T(8,128)(2,1)}, bf16[5,192,384]{2,1,0:T(8,128)(2,1)S(1)}, u32[]{:S(2)}, u32[]{:S(2)}) collective-permute-start(bf16[5,192,384]{2,1,0:T(8,128)(2,1)} %collective-permute-done.3), channel_id=1, source_target_pairs={{0,2},{2,4},{4,6},{6,8},{8,10},{10,12},{12,14},{14,0},{1,3},{3,5},... | collective-permute-start | bytes 2211848 | tf_op jit(solution)/shard_map/ppermute | solution.py:18
  83.6 16.2 %collective-permute-start = (bf16[1,2,1536]{2,1,0:T(2,128)(2,1)S(1)}, bf16[1,2,1536]{2,1,0:T(2,128)(2,1)S(1)}, u32[]{:S(2)}, u32[]{:S(2)}) collective-permute-start(bf16[1,2,1536]{2,1,0:T(2,128)(2,1)S(1)} %get-tuple-element.8), channel_id=1, source_target_pairs={{0,2},{2,4},{4,6},{6,8},{8,10},{10,12},{12,14},{1,3},{3,5},{5,7},{... | collective-permute-start | bytes 18440 | tf_op jit(solution)/shard_map/ppermute | solution.py:30
  86.9 18.1 %collective-permute-start.1 = (bf16[1,2,1536]{2,1,0:T(2,128)(2,1)S(1)}, bf16[1,2,1536]{2,1,0:T(2,128)(2,1)S(1)}, u32[]{:S(2)}, u32[]{:S(2)}) collective-permute-start(bf16[1,2,1536]{2,1,0:T(2,128)(2,1)S(1)} %get-tuple-element.7), channel_id=1, source_target_pairs={{2,0},{4,2},{6,4},{8,6},{10,8},{12,10},{14,12},{3,1},{5,3},{7,5},{... | collective-permute-start | bytes 18440 | tf_op jit(solution)/shard_map/ppermute | solution.py:33
  100.1 36.1 %collective-permute-start.7 = (bf16[5,192,384]{2,1,0:T(8,128)(2,1)}, bf16[5,192,384]{2,1,0:T(8,128)(2,1)S(1)}, u32[]{:S(2)}, u32[]{:S(2)}) collective-permute-start(bf16[5,192,384]{2,1,0:T(8,128)(2,1)} %collective-permute-done.6), channel_id=1, source_target_pairs={{0,14},{2,0},{4,2},{6,4},{8,6},{10,8},{12,10},{14,12},{1,15},{3,1}... | collective-permute-start | bytes 2211848 | tf_op jit(solution)/shard_map/ppermute | solution.py:20
  104.5 32.3 %collective-permute-start.5 = (bf16[5,192,384]{2,1,0:T(8,128)(2,1)S(1)}, bf16[5,192,384]{2,1,0:T(8,128)(2,1)S(1)}, u32[]{:S(2)}, u32[]{:S(2)}) collective-permute-start(bf16[5,192,384]{2,1,0:T(8,128)(2,1)S(1)} %collective-permute-done.4), channel_id=1, source_target_pairs={{0,2},{2,4},{4,6},{6,8},{8,10},{10,12},{12,14},{14,0},{1,3},{3,5},... | collective-permute-start | bytes 2211848 | tf_op jit(solution)/shard_map/ppermute | solution.py:18
  136.2 18.5 %collective-permute-start.8 = (bf16[5,192,384]{2,1,0:T(8,128)(2,1)S(1)}, bf16[5,192,384]{2,1,0:T(8,128)(2,1)S(1)}, u32[]{:S(2)}, u32[]{:S(2)}) collective-permute-start(bf16[5,192,384]{2,1,0:T(8,128)(2,1)S(1)} %collective-permute-done.7), channel_id=1, source_target_pairs={{0,14},{2,0},{4,2},{6,4},{8,6},{10,8},{12,10},{14,12},{1,15},{3,1}... | collective-permute-start | bytes 2211848 | tf_op jit(solution)/shard_map/ppermute | solution.py:20
  155.6 16.4 %copy-start.2 = (f32[384]{0:T(512)S(1)}, f32[384]{0:T(512)}, u32[]{:S(2)}) copy-start(f32[384]{0:T(512)} %param.17) | copy-start | bytes 4612
Sparse Core Ops, SparseCore 0:
  44.5 15.3 all-reduce.2
